TPU v7x, 32 devices: a whole 2x2x4 slice. The times are simulated.
32 devices in a mesh: dp: 4 (over x, core), fsdp: 8 (over z, y).
Axes of the slice: x: 2, y: 2, z: 4, core: 2. Of those that a mesh axis runs over, the one named last changes fastest.
Arguments:
- tokens: bfloat16 [8192, 2048], P(('dp', 'fsdp')), may hold values from -6 to 6
- w_q: bfloat16 [2048, 2048], P(('dp', 'fsdp')), may hold values from -0.125 to 0.125
- w_kv: bfloat16 [2048, 256], P(('dp', 'fsdp')), may hold values from -0.125 to 0.125
- g_attn: bfloat16 [2048], P(('dp', 'fsdp')), may hold values from 0.25 to 1.75
- g_mlp: bfloat16 [2048], P(('dp', 'fsdp')), may hold values from 0.25 to 1.75
- w_o: bfloat16 [2048, 2048], P(('dp', 'fsdp')), may hold values from -0.75 to 0.75
- w_gu: bfloat16 [5632, 2, 2048], P(('dp', 'fsdp')), may hold values from -0.125 to 0.125
- w_down: bfloat16 [5632, 2048], P(('dp', 'fsdp')), may hold values from -0.078125 to 0.078125
- grad_out: bfloat16 [8192, 2048], P(('dp', 'fsdp')), may hold values from -6 to 6
- grad_kv: bfloat16 [8192, 256], P(('dp', 'fsdp')), may hold values from -4 to 4
- group_id: int32 [32], P(('dp', 'fsdp')), may hold values from 0 to 7
- group_size: int32 [8], replicated, may hold values from 1 to 4
- group_weight: float32 [8], replicated, may hold values from 1 to 4
Outputs:
- output: bfloat16 [8192, 2048], P(('dp', 'fsdp'))
- d_tokens: float32 [8192, 2048], P(('dp', 'fsdp'))
- kv_out: bfloat16 [8192, 256], P(('dp', 'fsdp'))
- d_kv: float32 [8192, 256], P(('dp', 'fsdp'))
- d_w_q: float32 [2048, 2048], P(('dp', 'fsdp'))
- d_w_kv: float32 [2048, 256], P(('dp', 'fsdp'))
- d_g_attn: float32 [2048], P(('dp', 'fsdp'))
- d_g_mlp: float32 [2048], P(('dp', 'fsdp'))
- d_w_o: float32 [2048, 2048], P(('dp', 'fsdp'))
- d_w_gu: float32 [5632, 2, 2048], P(('dp', 'fsdp'))
- d_w_down: float32 [5632, 2048], P(('dp', 'fsdp'))
All inputs are finite; a program needn't handle non-finite values.
Results may differ from a plain program's by a relative error of at most 0.015.
Values may be sent and summed in bfloat16 or wider, within the bound.
No kernel may reach another device: no remote copies, remote signals or barrier semaphores. Data moves between devices by JAX's collectives and lax.ppermute only.
A program may use at most 256 MiB of HBM per device.

v0:
```python
import jax
import jax.numpy as jnp
from jax import lax
from jax.sharding import PartitionSpec as P

epsilon = 1e-05
theta_base = 10000.0


def rope_tables(length, width):
    halfway = width // 2
    freqs = theta_base ** (-(jnp.arange(halfway, dtype=jnp.float32) * 2.0 / width))
    angles = jnp.arange(length, dtype=jnp.float32)[:, None] * freqs[None, :]
    return (jnp.cos(angles), jnp.sin(angles))


def rotate(vectors, cosines, sine_part):
    halfway = vectors.shape[-1] // 2
    front = vectors[..., :halfway]
    behind = vectors[..., halfway:]
    return jnp.concatenate(
        [front * cosines - behind * sine_part, behind * cosines + front * sine_part], axis=-1
    )


def contract_last(left, right):
    return lax.dot_general(
        left,
        right,
        (((left.ndim - 1,), (right.ndim - 1,)), ((), ())),
        preferred_element_type=jnp.float32,
    )


def contract_first(left, right):
    return lax.dot_general(
        left, right, (((0,), (0,)), ((), ())), preferred_element_type=jnp.float32
    )


def local(
    tokens,
    w_q,
    w_kv,
    g_attn,
    g_mlp,
    w_o,
    w_gu,
    w_down,
    grad_out,
    grad_kv,
    group_id,
    group_size,
    group_weight,
):
    length, width = tokens.shape
    head_dim = grad_kv.shape[1] // 2
    q_width = w_q.shape[1]
    head_count = q_width // head_dim
    matches = jnp.arange(group_size.shape[0], dtype=jnp.int32) == group_id[0]
    factor = jnp.sum(jnp.where(matches, group_weight / group_size.astype(jnp.float32), 0.0))
    cosines, sine_part = rope_tables(length, head_dim)
    x_full = tokens.astype(jnp.float32)
    inv_one = lax.rsqrt(jnp.mean(x_full * x_full, axis=-1, keepdims=True) + epsilon)
    normed_one = x_full * inv_one
    wq_piece = lax.all_gather(w_q, ("dp", "fsdp"), axis=0, tiled=True)
    wkv_piece = lax.all_gather(w_kv, ("dp", "fsdp"), axis=0, tiled=True)
    gain_piece = lax.all_gather(g_attn, ("dp", "fsdp"), axis=0, tiled=True)
    mlp_gain_piece = lax.all_gather(g_mlp, ("dp", "fsdp"), axis=0, tiled=True)
    normed_cols = normed_one
    h_cols = (normed_cols * gain_piece.astype(jnp.float32)).astype(jnp.bfloat16)
    q_acc = jnp.dot(h_cols, wq_piece, preferred_element_type=jnp.float32)
    kv_acc = jnp.dot(h_cols, wkv_piece, preferred_element_type=jnp.float32)
    gain_two = mlp_gain_piece.astype(jnp.float32)
    q_pre, kv_pre, gain_two, h_one = (q_acc, kv_acc, gain_two, h_cols)
    q_low = rotate(
        q_pre.reshape(length, head_count, head_dim), cosines[:, None, :], sine_part[:, None, :]
    ).astype(jnp.bfloat16)
    k_low = rotate(kv_pre[:, :head_dim], cosines, sine_part).astype(jnp.bfloat16)
    v_low = kv_pre[:, head_dim:].astype(jnp.bfloat16)
    score_scale = head_dim ** (-0.5)
    causal = jnp.arange(length)[:, None] >= jnp.arange(length)[None, :]

    def logits_of(queries, keys):
        raw_scores = jnp.einsum("thd,sd->hts", queries, keys, preferred_element_type=jnp.float32)
        return jnp.where(causal[None], raw_scores * score_scale, -1e30)

    logits = logits_of(q_low, k_low)
    row_top = jnp.max(logits, axis=-1, keepdims=True)
    exp_vals = jnp.exp(logits - row_top)
    row_total = jnp.sum(exp_vals, axis=-1, keepdims=True)
    prob_full = exp_vals / row_total
    log_total = row_top + jnp.log(row_total)
    prob_low = prob_full.astype(jnp.bfloat16)
    attended = jnp.einsum("hts,sd->thd", prob_low, v_low, preferred_element_type=jnp.float32)
    attn_low = attended.reshape(length, q_width).astype(jnp.bfloat16)
    branch = jnp.dot(
        attn_low,
        lax.all_gather(w_o, ("dp", "fsdp"), axis=0, tiled=True),
        preferred_element_type=jnp.float32,
    )
    x_mid = x_full + branch
    inv_two = lax.rsqrt(jnp.mean(x_mid * x_mid, axis=-1, keepdims=True) + epsilon)
    normed_two = x_mid * inv_two
    h_two = (normed_two * gain_two).astype(jnp.bfloat16)
    grad_top = grad_out.astype(jnp.float32) * factor
    grad_low = grad_top.astype(jnp.bfloat16)
    ff_rows, grad_rows = (
        lax.all_gather(h_two, "dp", axis=0, tiled=True),
        lax.all_gather(grad_low, "dp", axis=0, tiled=True),
    )
    gu_piece = lax.all_gather(w_gu, "fsdp", axis=0, tiled=True)
    down_piece = lax.all_gather(w_down, "fsdp", axis=0, tiled=True)
    both_proj = jnp.einsum("td,fkd->tkf", ff_rows, gu_piece, preferred_element_type=jnp.float32)
    gate_vals = both_proj[:, 0]
    up_vals = both_proj[:, 1]
    hid_cols = (jax.nn.silu(gate_vals) * up_vals).astype(jnp.bfloat16)
    mlp_out = jnp.dot(hid_cols, down_piece, preferred_element_type=jnp.float32)
    mlp_part = mlp_out
    gate_all = gate_vals
    up_all = up_vals
    mlp_out = lax.psum_scatter(
        mlp_part.astype(jnp.bfloat16), "dp", scatter_dimension=0, tiled=True
    ).astype(jnp.float32)
    gu_piece = lax.all_gather(w_gu, "fsdp", axis=0, tiled=True)
    down_piece = lax.all_gather(w_down, "fsdp", axis=0, tiled=True)
    gate_vals = gate_all
    up_vals = up_all
    d_hid = contract_last(grad_rows, down_piece)
    sigmoid_vals = jax.nn.sigmoid(gate_vals)
    d_gate = d_hid * up_vals * sigmoid_vals * (1.0 + gate_vals * (1.0 - sigmoid_vals))
    d_up = d_hid * gate_vals * sigmoid_vals
    d_both = jnp.stack([d_gate, d_up], axis=1).astype(jnp.bfloat16)
    d_h_two = jnp.einsum("tkf,fkd->td", d_both, gu_piece, preferred_element_type=jnp.float32)
    d_h_part = d_h_two
    d_h_two = lax.psum_scatter(
        d_h_part.astype(jnp.bfloat16), "dp", scatter_dimension=0, tiled=True
    ).astype(jnp.float32)
    d_w_down = lax.psum_scatter(
        contract_first(hid_cols, grad_rows).astype(jnp.bfloat16),
        "fsdp",
        scatter_dimension=0,
        tiled=True,
    ).astype(jnp.float32)
    d_w_gu = lax.psum_scatter(
        jnp.einsum("tkf,td->fkd", d_both, ff_rows, preferred_element_type=jnp.float32).astype(
            jnp.bfloat16
        ),
        "fsdp",
        scatter_dimension=0,
        tiled=True,
    ).astype(jnp.float32)
    output = (x_mid + mlp_out).astype(jnp.bfloat16)
    d_gain_two = jnp.sum(d_h_two * normed_two, axis=0)
    d_normed_two = d_h_two * gain_two
    d_mid = grad_top + inv_two * (
        d_normed_two - normed_two * jnp.mean(d_normed_two * normed_two, axis=-1, keepdims=True)
    )
    d_mid_low = d_mid.astype(jnp.bfloat16)
    d_attended = contract_last(d_mid_low, lax.all_gather(w_o, ("dp", "fsdp"), axis=0, tiled=True))
    d_att_low = d_attended.astype(jnp.bfloat16).reshape(length, head_count, head_dim)
    d_w_o = lax.psum_scatter(
        contract_first(attn_low, d_mid_low), ("dp", "fsdp"), scatter_dimension=0, tiled=True
    )
    prob_back = jnp.exp(logits_of(q_low, k_low) - log_total)
    prob_back_low = prob_back.astype(jnp.bfloat16)
    d_probs = jnp.einsum("thd,sd->hts", d_att_low, v_low, preferred_element_type=jnp.float32)
    d_v_own = jnp.einsum(
        "hts,thd->sd", prob_back_low, d_att_low, preferred_element_type=jnp.float32
    )
    d_logit = prob_back * (d_probs - jnp.sum(prob_back * d_probs, axis=-1, keepdims=True))
    d_raw = (d_logit * score_scale).astype(jnp.bfloat16)
    d_q_rot = jnp.einsum("hts,sd->thd", d_raw, k_low, preferred_element_type=jnp.float32)
    d_k_own = jnp.einsum("hts,thd->sd", d_raw, q_low, preferred_element_type=jnp.float32)
    kv_extra = grad_kv.astype(jnp.float32) * factor
    d_k_total = d_k_own + kv_extra[:, :head_dim]
    d_v_total = d_v_own + kv_extra[:, head_dim:]
    d_kv = jnp.concatenate([d_k_total, d_v_total], axis=1)
    d_kv_low = jnp.concatenate([rotate(d_k_total, cosines, -sine_part), d_v_total], axis=1).astype(
        jnp.bfloat16
    )
    d_q_low = (
        rotate(d_q_rot, cosines[:, None, :], -sine_part[:, None, :])
        .reshape(length, q_width)
        .astype(jnp.bfloat16)
    )
    wq_piece = lax.all_gather(w_q, ("dp", "fsdp"), axis=0, tiled=True)
    wkv_piece = lax.all_gather(w_kv, ("dp", "fsdp"), axis=0, tiled=True)
    gain_piece = lax.all_gather(g_attn, ("dp", "fsdp"), axis=0, tiled=True)
    d_h_cols = contract_last(d_q_low, wq_piece) + contract_last(d_kv_low, wkv_piece)
    normed_cols = normed_one
    d_normed = d_h_cols * gain_piece.astype(jnp.float32)
    d_gain = jnp.sum(d_h_cols * normed_cols, axis=0)
    d_tokens = d_mid + inv_one * (
        d_normed - normed_one * jnp.mean(d_normed * normed_one, axis=-1, keepdims=True)
    )
    joined = jnp.concatenate([d_q_low, d_kv_low], axis=1)
    d_w_in = lax.psum_scatter(
        contract_first(h_one, joined), ("dp", "fsdp"), scatter_dimension=0, tiled=True
    )
    d_g_attn, d_g_mlp = (
        lax.psum_scatter(d_gain, ("dp", "fsdp"), scatter_dimension=0, tiled=True),
        lax.psum_scatter(d_gain_two, ("dp", "fsdp"), scatter_dimension=0, tiled=True),
    )
    kv_out = jnp.concatenate([k_low, v_low], axis=1)
    return (
        output,
        d_tokens,
        kv_out,
        d_kv,
        d_w_in[:, :q_width],
        d_w_in[:, q_width:],
        d_g_attn,
        d_g_mlp,
        d_w_o,
        d_w_gu,
        d_w_down,
    )


def solution(mesh):
    placed = (
        P(("dp", "fsdp"), None),
        P(("dp", "fsdp"), None),
        P(("dp", "fsdp"), None),
        P(("dp", "fsdp")),
        P(("dp", "fsdp")),
        P(("dp", "fsdp"), None),
        P(("dp", "fsdp"), None, None),
        P(("dp", "fsdp"), None),
        P(("dp", "fsdp"), None),
        P(("dp", "fsdp"), None),
        P(("dp", "fsdp")),
        P(),
        P(),
    )
    return jax.shard_map(
        local,
        mesh=mesh,
        in_specs=placed,
        out_specs=(
            P(("dp", "fsdp"), None),
            P(("dp", "fsdp"), None),
            P(("dp", "fsdp"), None),
            P(("dp", "fsdp"), None),
            P(("dp", "fsdp"), None),
            P(("dp", "fsdp"), None),
            P(("dp", "fsdp")),
            P(("dp", "fsdp")),
            P(("dp", "fsdp"), None),
            P(("dp", "fsdp"), None, None),
            P(("dp", "fsdp"), None),
        ),
        check_vma=False,
    )
```

profile of v0, /device:TPU:0, one launch (start us, length us, event | category | flops | bytes accessed | tf_op | source)
XLA Modules:
  0.0 1734.8 jit_solution(2765132462502652689)
XLA Ops:
  7.3 0.7 all-gather.8.cloned.1.call-update
  8.0 0.7 all-gather.10.cloned.1.call-update
  9.5 3.0 copy.76
  13.1 42.2 %all-reduce.6 = (bf16[2048]{0:T(1024)(128)(2,1)S(1)}, bf16[2048]{0:T(1024)(128)(2,1)S(1)}) all-reduce(bf16[2048]{0:T(1024)(128)(2,1)S(1)} %dynamic-update-slice, bf16[2048]{0:T(1024)(128)(2,1)S(1)} %dynamic-update-slice.1), channel_id=1, replica_groups=mesh['dp'=4,'fsdp'=8] {'dp','fsdp'}, use_global_device_ids=true, to_apply=%add | all-reduce | flops 4096 | bytes 16384
  55.6 12.1 all-gather.8.cloned.1.call-done
  67.8 1.9 fusion.81
  70.2 76.8 %all-gather.10.cloned.1.call-done = bf16[2048,2048]{1,0:T(8,128)(2,1)} async-done(((bf16[64,2048]{1,0:T(8,128)(2,1)}), bf16[2048,2048]{1,0:T(8,128)(2,1)}) %all-gather.10.cloned.1.call-update) | async-done | bytes 8388624 | tf_op jit(solution)/shard_map/all_gather | solution.py:66
  147.0 5.8 convolution_bitcast_fusion.1
  153.9 1.4 subtract_convert_fusion.1
  155.3 1.3 fusion.84
  157.3 1.4 copy-done
  158.7 2.0 fusion.36
  160.6 65.3 %all-gather.12.cloned.1.call-done = bf16[2048,2048]{1,0:T(8,128)(2,1)} async-done(((bf16[64,2048]{1,0:T(8,128)(2,1)}), bf16[2048,2048]{1,0:T(8,128)(2,1)}) %all-gather.12.cloned.1.call-update) | async-done | bytes 8388624 | tf_op jit(solution)/shard_map/all_gather | solution.py:99
  225.9 6.2 multiply_reduce_fusion
  232.1 1.2 multiply_convert_fusion.3
  234.7 3.2 fusion.33
  238.0 0.7 all-gather.18.cloned.1.call-update
  239.1 151.7 %all-gather.16.cloned.1.call-done = bf16[1408,2,2048]{2,0,1:T(8,128)(2,1)} async-done(((bf16[176,2,2048]{2,0,1:T(8,128)(2,1)}), bf16[1408,2,2048]{2,0,1:T(8,128)(2,1)}) %all-gather.16.cloned.1.call-update) | async-done | bytes 11534352 | tf_op jit(solution)/shard_map/all_gather | solution.py:112
  390.8 34.7 %all-gather.14.cloned.1.call-done = bf16[1024,2048]{1,0:T(8,128)(2,1)} async-done(((bf16[256,2048]{1,0:T(8,128)(2,1)}), bf16[1024,2048]{1,0:T(8,128)(2,1)}) %all-gather.14.cloned.1.call-update) | async-done | bytes 4194320 | tf_op jit(solution)/shard_map/all_gather | solution.py:109
  425.5 18.8 %convolution_bitcast_fusion = f32[1024,2,1408]{2,0,1:T(8,128)} fusion(bf16[1408,2,2048]{2,0,1:T(8,128)(2,1)} %all-gather.16.cloned.1.call-done, bf16[1024,2048]{1,0:T(8,128)(2,1)} %all-gather.14.cloned.1.call-done), kind=kOutput, calls=%fused_computation.4 | convolution fusion | flops 11811160064 | bytes 27262976 | tf_op jit(solution)/shard_map/td,fkd->tkf/dot_general | solution.py:114
  444.3 17.7 %all-gather.20.cloned.1.call-done = bf16[1024,2048]{1,0:T(8,128)(2,1)} async-done(((bf16[256,2048]{1,0:T(8,128)(2,1)}), bf16[1024,2048]{1,0:T(8,128)(2,1)}) %all-gather.20.cloned.1.call-update) | async-done | bytes 4194320 | tf_op jit(solution)/shard_map/all_gather | solution.py:110
  462.0 94.9 %all-gather.18.cloned.1.call-done = bf16[1408,2048]{1,0:T(8,128)(2,1)} async-done(((bf16[176,2048]{1,0:T(8,128)(2,1)}), bf16[1408,2048]{1,0:T(8,128)(2,1)}) %all-gather.18.cloned.1.call-update) | async-done | bytes 5767184 | tf_op jit(solution)/shard_map/all_gather | solution.py:113
  556.9 15.6 fusion.13
  572.5 1.6 copy-done.30
  574.1 0.9 copy-done.31
  575.0 16.3 bitcast_convert_fusion
  591.6 10.9 convolution_convert_fusion.1
  602.6 10.5 convolution_convert_fusion
  613.2 18.3 %convert_bitcast_fusion = bf16[1408,2,2048]{0,2,1:T(8,128)(2,1)} fusion(bf16[1024,2048]{1,0:T(8,128)(2,1)} %all-gather.14.cloned.1.call-done, bf16[1024,1,1408]{2,0,1:T(8,128)(2,1)} %copy-done.31, bf16[1024,1,1408]{2,0,1:T(8,128)(2,1)} %copy-done.30), kind=kOutput, calls=%fused_computation.1 | convolution fusion | flops 11828461568 | bytes 21495808 | tf_op jit(solution)/shard_map/tkf,td->fkd/dot_general | solution.py:146
  631.6 29.4 %copy.89 = bf16[1408,2,2048]{2,1,0:T(2,128)(2,1)} copy(bf16[1408,2,2048]{0,2,1:T(8,128)(2,1)} %convert_bitcast_fusion) | data formatting | bytes 23068672 | tf_op jit(solution)/shard_map/convert_element_type | solution.py:146
  661.9 0.8 copy.85
  662.6 1.6 convert_multiply_fusion.5
  664.2 1.4 log_add_fusion
  665.6 2.6 fusion.19
  668.8 12.7 reduce-scatter.6.cloned.1.call-done
  681.5 4.4 fusion.18
  685.9 1.3 copy-done.2
  687.3 5.7 convolution_convert_fusion.2
  693.6 3.7 fusion.61
  697.2 9.2 fusion.49
  706.5 1.2 subtract_convert_fusion.2
  707.8 9.5 fusion.35
  717.3 3.2 subtract_convert_fusion
  720.4 1.6 pad_maximum_fusion.4
  722.0 1.5 copy.82
  723.5 4.1 fusion.85
  727.6 8.2 fusion.37
  736.1 1.3 copy-done.3
  737.4 9.3 fusion.53
  748.6 0.9 slice.112
  749.6 0.8 copy.90
  750.3 1.0 pad_maximum_fusion.5
  751.3 0.8 copy.91
  752.2 6.2 fusion.88
  758.4 2.3 fusion.25
  760.6 42.5 %all-reduce.5 = (f32[2048]{0:T(1024)S(1)}, f32[2048]{0:T(1024)S(1)}) all-reduce(f32[2048]{0:T(1024)S(1)} %get-tuple-element.46, f32[2048]{0:T(1024)S(1)} %copy-done.21), channel_id=5, replica_groups=mesh['dp'=4,'fsdp'=8] {'dp','fsdp'}, use_global_device_ids=true, to_apply=%region_12.13.clone | all-reduce | flops 4096 | bytes 32768
  804.3 4.1 fusion.24
  808.4 2.4 convert_element_type.122
  810.8 345.1 %all-reduce.9.cloned.1.call-done = bf16[1408,2,2048]{2,1,0:T(2,128)(2,1)} async-done(((bf16[1408,2,2048]{2,1,0:T(2,128)(2,1)}), bf16[1408,2,2048]{2,1,0:T(2,128)(2,1)}) %all-reduce.9.cloned.1.call-update) | async-done | bytes 11534352
  1155.9 4.6 dynamic-slice_convert_fusion
  1160.5 207.4 %reduce-scatter.10.cloned.1.call-done = f32[64,2304]{1,0:T(8,128)} async-done(((f32[2048,2304]{1,0:T(8,128)}), f32[64,2304]{1,0:T(8,128)}) %reduce-scatter.10.cloned.1.call-update) | async-done | bytes 589840 | tf_op jit(solution)/shard_map/reduce_scatter | solution.py:198
  1367.9 1.9 slice.77
  1369.8 1.5 slice.78
  1371.3 356.5 %reduce-scatter.12.cloned.1.call-done = f32[64,2048]{1,0:T(8,128)} async-done(((f32[2048,2048]{1,0:T(8,128)}), f32[64,2048]{1,0:T(8,128)}) %reduce-scatter.12.cloned.1.call-update) | async-done | bytes 524304 | tf_op jit(solution)/shard_map/reduce_scatter | solution.py:162
  (110 shorter events, 10.2 us)
Async XLA Ops:
  7.2 5.4 copy-start.27
  7.2 5.7 copy-start.28
  7.2 48.1 %copy-start.1 = (bf16[256,2048]{1,0:T(8,128)(2,1)S(1)}, bf16[256,2048]{1,0:T(8,128)(2,1)}, u32[]{:S(2)}) copy-start(bf16[256,2048]{1,0:T(8,128)(2,1)} %param.13) | copy-start | bytes 3145732
  7.2 60.6 %all-gather.8.cloned.1.call-start = ((), (), s32[]{:S(2)}) async-start(), calls=%async_computation.5 | async-start | bytes 1081344 | tf_op jit(solution)/shard_map/all_gather | solution.py:67
  7.9 139.1 %all-gather.10.cloned.1.call-start = ((), (), s32[]{:S(2)}) async-start(), calls=%async_computation.6 | async-start | bytes 8650752 | tf_op jit(solution)/shard_map/all_gather | solution.py:66
  8.7 217.2 %all-gather.12.cloned.1.call-start = ((), (), s32[]{:S(2)}) async-start(), calls=%async_computation.7 | async-start | bytes 8650752 | tf_op jit(solution)/shard_map/all_gather | solution.py:99
  9.4 381.4 %all-gather.16.cloned.1.call-start = ((), (), s32[]{:S(2)}) async-start(), calls=%async_computation.9 | async-start | bytes 12976128 | tf_op jit(solution)/shard_map/all_gather | solution.py:112
  12.5 413.0 %all-gather.14.cloned.1.call-start = ((), (), s32[]{:S(2)}) async-start(), calls=%async_computation.8 | async-start | bytes 5242880 | tf_op jit(solution)/shard_map/all_gather | solution.py:109
  55.3 14.7 copy-start.23
  55.6 97.2 %copy-start.19 = (f32[256]{0:T(256)}, f32[256]{0:T(256)S(1)}, u32[]{:S(2)}) copy-start(f32[256]{0:T(256)S(1)} %add_rsqrt_fusion.1) | copy-start | bytes 3076
  69.6 87.6 %copy-start.11 = (f32[256,256]{0,1:T(8,128)}, f32[256,256]{0,1:T(8,128)S(1)}, u32[]{:S(2)}) copy-start(f32[256,256]{0,1:T(8,128)S(1)} %fusion.81) | copy-start | bytes 786436
  70.0 85.3 %copy-start.12 = (bf16[256,64]{0,1:T(8,128)(2,1)}, bf16[256,64]{0,1:T(8,128)(2,1)S(1)}, u32[]{:S(2)}) copy-start(bf16[256,64]{0,1:T(8,128)(2,1)S(1)} %get-tuple-element.63) | copy-start | bytes 98308
  70.0 85.3 %copy-start.14 = (bf16[256,64]{0,1:T(8,128)(2,1)}, bf16[256,64]{0,1:T(8,128)(2,1)S(1)}, u32[]{:S(2)}) copy-start(bf16[256,64]{0,1:T(8,128)(2,1)S(1)} %get-tuple-element.64) | copy-start | bytes 98308
  155.2 1.4 copy-start.4
  155.2 1.4 copy-start.6
  156.7 2.0 copy-start
  156.7 4.0 copy-start.16
  158.7 2.0 copy-start.18
  232.1 2.0 copy-start.25
  232.1 2.0 copy-start.26
  232.1 5.8 copy-start.22
  233.4 228.6 %all-gather.20.cloned.1.call-start = ((), (), s32[]{:S(2)}) async-start(), calls=%async_computation.12 | async-start | bytes 5242880 | tf_op jit(solution)/shard_map/all_gather | solution.py:110
  237.9 318.9 %all-gather.18.cloned.1.call-start = ((), (), s32[]{:S(2)}) async-start(), calls=%async_computation.10 | async-start | bytes 6488064 | tf_op jit(solution)/shard_map/all_gather | solution.py:113
  238.7 427.0 %reduce-scatter.8.cloned.1.call-start = ((), (), s32[]{:S(2)}) async-start(), calls=%async_computation.13 | async-start | bytes 5242880 | tf_op jit(solution)/shard_map/reduce_scatter | solution.py:136
  572.5 1.6 copy-start.30
  572.5 2.5 copy-start.31
  591.4 90.1 %reduce-scatter.6.cloned.1.call-start = ((), (), s32[]{:S(2)}) async-start(), calls=%async_computation.11 | async-start | bytes 5242880 | tf_op jit(solution)/shard_map/reduce_scatter | solution.py:122
  602.6 205.8 %reduce-scatter.14.cloned.1.call-start = ((), (), s32[]{:S(2)}) async-start(), calls=%async_computation.16 | async-start | bytes 6488064 | tf_op jit(solution)/shard_map/reduce_scatter | solution.py:139
  613.2 542.7 %all-reduce.9.cloned.1.call-start = ((), (), s32[]{:S(2)}) async-start(), calls=%async_computation.17 | async-start | bytes 23068672
  661.0 0.9 copy-start.17
  661.0 706.9 %reduce-scatter.10.cloned.1.call-start = ((), (), s32[]{:S(2)}) async-start(), calls=%async_computation.14 | async-start | bytes 19464192 | tf_op jit(solution)/shard_map/reduce_scatter | solution.py:198
  664.2 33.0 %copy-start.9 = (f32[256,256]{0,1:T(8,128)}, f32[256,256]{0,1:T(8,128)S(1)}, u32[]{:S(2)}) copy-start(f32[256,256]{0,1:T(8,128)S(1)} %convert_multiply_fusion.5) | copy-start | bytes 786436
  685.9 1.3 copy-start.2
  693.5 3.7 copy-start.5
  697.2 9.3 copy-start.24
  720.4 3.1 copy-start.10
  723.5 12.3 copy-start.7
  723.5 4.1 copy-start.20
  735.8 1.6 copy-start.3
  735.8 992.0 %reduce-scatter.12.cloned.1.call-start = ((), (), s32[]{:S(2)}) async-start(), calls=%async_computation.15 | async-start | bytes 17301504 | tf_op jit(solution)/shard_map/reduce_scatter | solution.py:162
  746.7 0.7 copy-start.29
  746.7 2.8 copy-start.13
  746.7 2.8 copy-start.15
  752.2 6.2 copy-start.8
  758.4 2.3 copy-start.21
Sparse Core Ops, SparseCore 0:
  11.1 56.5 all-gather.7
  70.7 76.2 all-gather.9
  150.0 75.8 all-gather.11
  228.5 162.2 all-gather.15
  392.8 32.6 all-gather.13
  427.5 34.4 all-gather.19
  464.2 92.6 all-gather.17
  591.5 42.6 reduce-scatter.7
  636.9 44.5 reduce-scatter.5
  685.0 111.5 reduce-scatter.13
  800.5 355.3 all-reduce.8
  1162.1 205.7 reduce-scatter.9
  1370.8 356.9 reduce-scatter.11
where the time goes:
time: 1750 us; the launch traced here: 1730 us
  waiting for transfers between devices  1380 us (79%)
  matrix products  166 us (9%)
  blocking collectives  84.7 us (5%)
  local copies, waits for them, and re-layouts  52.5 us (3%)
  other arithmetic  36.2 us (2%)
    reduce_scatter x1, waiting for transfers between devices, local(): lax.psum_scatter(contract_first(attn_low, d_mid_low), ('dp', 'fsdp'), sca...  357 us
    unnamed x14, waiting for transfers between devices  348 us
    reduce_scatter x1, waiting for transfers between devices, local(): lax.psum_scatter(contract_first(h_one, joined), ('dp', 'fsdp'), scatter_d...  207 us
    all_gather x1, waiting for transfers between devices, local(): gu_piece = lax.all_gather(w_gu, 'fsdp', axis=0, tiled=True)  152 us
    all_gather x1, waiting for transfers between devices, local(): down_piece = lax.all_gather(w_down, 'fsdp', axis=0, tiled=True)  94.9 us
    unnamed x2, blocking collectives  84.7 us
    all_gather x1, waiting for transfers between devices, local(): wq_piece = lax.all_gather(w_q, ('dp', 'fsdp'), axis=0, tiled=True)  76.8 us
    all_gather x1, waiting for transfers between devices, local(): lax.all_gather(w_o, ('dp', 'fsdp'), axis=0, tiled=True)  65.3 us
  transfers between devices with their start and end apart: 13, of which 11 were waited for; matrix products, arithmetic and copies ran while one was open for 12% of the time, Pallas kernels for 0%

commit v1 on v0

--- a/solution.py
+++ b/solution.py
@@ -1,3 +1,4 @@
+import functools
 import jax
 import jax.numpy as jnp
 from jax import lax
@@ -5,6 +6,31 @@
 
 epsilon = 1e-05
 theta_base = 10000.0
+
+
+def apply_sheets(x_part, which_axis):
+    z, even, met_up = (lax.axis_size(which_axis), lax.axis_index(which_axis), x_part.shape[0])
+    heard = lax.dynamic_update_slice_in_dim(
+        jnp.zeros([ii * z if j0 == 0 else ii for j0, ii in enumerate(x_part.shape)], x_part.dtype),
+        x_part,
+        even * met_up,
+        axis=0,
+    )
+    block_out = latest = x_part
+    for src_i in [*range(1, z // 2 + 1)]:
+        block_out = lax.ppermute(block_out, which_axis, [(j0, (j0 + 1) % z) for j0 in range(z)])
+        heard = lax.dynamic_update_slice_in_dim(
+            heard, block_out, (even - src_i) % z * met_up, axis=0
+        )
+        if 2 * src_i < z:
+            latest = lax.ppermute(latest, which_axis, [(j0, (j0 - 1) % z) for j0 in range(z)])
+            heard = lax.dynamic_update_slice_in_dim(
+                heard, latest, (even + src_i) % z * met_up, axis=0
+            )
+    return heard
+
+
+map_the_core = functools.partial(apply_sheets, which_axis="fsdp")
 
 
 def rope_tables(length, width):
@@ -110,7 +136,7 @@
         lax.all_gather(grad_low, "dp", axis=0, tiled=True),
     )
     gu_piece = lax.all_gather(w_gu, "fsdp", axis=0, tiled=True)
-    down_piece = lax.all_gather(w_down, "fsdp", axis=0, tiled=True)
+    down_piece = map_the_core(w_down)
     both_proj = jnp.einsum("td,fkd->tkf", ff_rows, gu_piece, preferred_element_type=jnp.float32)
     gate_vals = both_proj[:, 0]
     up_vals = both_proj[:, 1]

time: 1750 us -> 1820 us (1.040)
  waiting for transfers between devices: 1380 us -> 1440 us
    ppermute x0 -> x7, waiting for transfers between devices: none -> 92.4 us  [the longest x4 92 us: apply_sheets(): lax.ppermute(block_out, which_axis, [(j0, (j0 + 1) % z) for j0 in range(z)])]
    unnamed x14, waiting for transfers between devices: 348 us -> 326 us
  transfers between devices with their start and end apart: 13 -> 20, of which waited for: 11 -> 15; matrix products, arithmetic and copies ran while one was open for 12% -> 12% of each run, Pallas kernels for 0% -> 0%
where the time goes in v1:
time: 1820 us; the launch traced here: 1810 us
  waiting for transfers between devices  1440 us (79%)
  matrix products  165 us (9%)
  blocking collectives  81.5 us (4%)
  local copies, waits for them, and re-layouts  58.4 us (3%)
  other arithmetic  35.3 us (2%)
  starting transfers between devices  18.2 us (1%)
    reduce_scatter x1, waiting for transfers between devices, local(): lax.psum_scatter(contract_first(attn_low, d_mid_low), ('dp', 'fsdp'), sca...  357 us
    unnamed x14, waiting for transfers between devices  326 us
    reduce_scatter x1, waiting for transfers between devices, local(): lax.psum_scatter(contract_first(h_one, joined), ('dp', 'fsdp'), scatter_d...  207 us
    all_gather x1, waiting for transfers between devices, local(): gu_piece = lax.all_gather(w_gu, 'fsdp', axis=0, tiled=True)  152 us
    all_gather x1, waiting for transfers between devices, local(): down_piece = lax.all_gather(w_down, 'fsdp', axis=0, tiled=True)  94.9 us
    ppermute x4, waiting for transfers between devices, apply_sheets(): lax.ppermute(block_out, which_axis, [(j0, (j0 + 1) % z) for j0 in range(z)])  92 us
    unnamed x2, blocking collectives  81.5 us
    all_gather x1, waiting for transfers between devices, local(): wq_piece = lax.all_gather(w_q, ('dp', 'fsdp'), axis=0, tiled=True)  76.8 us
  transfers between devices with their start and end apart: 20, of which 15 were waited for; matrix products, arithmetic and copies ran while one was open for 12% of the time, Pallas kernels for 0%

profile of v1, /device:TPU:0, one launch (start us, length us, event | category | flops | bytes accessed | tf_op | source)
XLA Modules:
  0.0 1809.9 jit_solution(4096346867762497731)
XLA Ops:
  9.5 3.0 copy.76
  13.1 42.1 %all-reduce.6 = (bf16[2048]{0:T(1024)(128)(2,1)S(1)}, bf16[2048]{0:T(1024)(128)(2,1)S(1)}) all-reduce(bf16[2048]{0:T(1024)(128)(2,1)S(1)} %dynamic-update-slice, bf16[2048]{0:T(1024)(128)(2,1)S(1)} %dynamic-update-slice.1), channel_id=1, replica_groups=mesh['dp'=4,'fsdp'=8] {'dp','fsdp'}, use_global_device_ids=true, to_apply=%add | all-reduce | flops 4096 | bytes 16384
  56.2 11.6 all-gather.8.cloned.1.call-done
  67.8 1.9 fusion.81
  70.2 76.8 %all-gather.10.cloned.1.call-done = bf16[2048,2048]{1,0:T(8,128)(2,1)} async-done(((bf16[64,2048]{1,0:T(8,128)(2,1)}), bf16[2048,2048]{1,0:T(8,128)(2,1)}) %all-gather.10.cloned.1.call-update) | async-done | bytes 8388624 | tf_op jit(solution)/shard_map/all_gather | solution.py:92
  147.0 5.8 convolution_bitcast_fusion.1
  153.9 1.4 subtract_convert_fusion.1
  155.3 1.3 fusion.84
  157.2 1.4 copy-done
  158.6 2.0 fusion.36
  160.6 65.4 %all-gather.12.cloned.1.call-done = bf16[2048,2048]{1,0:T(8,128)(2,1)} async-done(((bf16[64,2048]{1,0:T(8,128)(2,1)}), bf16[2048,2048]{1,0:T(8,128)(2,1)}) %all-gather.12.cloned.1.call-update) | async-done | bytes 8388624 | tf_op jit(solution)/shard_map/all_gather | solution.py:125
  226.1 6.2 multiply_reduce_fusion
  234.9 3.2 fusion.33
  238.9 152.1 %all-gather.16.cloned.1.call-done = bf16[1408,2,2048]{2,0,1:T(8,128)(2,1)} async-done(((bf16[176,2,2048]{2,0,1:T(8,128)(2,1)}), bf16[1408,2,2048]{2,0,1:T(8,128)(2,1)}) %all-gather.16.cloned.1.call-update) | async-done | bytes 11534352 | tf_op jit(solution)/shard_map/all_gather | solution.py:138
  390.9 34.7 %all-gather.14.cloned.1.call-done = bf16[1024,2048]{1,0:T(8,128)(2,1)} async-done(((bf16[256,2048]{1,0:T(8,128)(2,1)}), bf16[1024,2048]{1,0:T(8,128)(2,1)}) %all-gather.14.cloned.1.call-update) | async-done | bytes 4194320 | tf_op jit(solution)/shard_map/all_gather | solution.py:135
  425.6 19.2 %convolution_bitcast_fusion = f32[1024,2,1408]{2,0,1:T(8,128)} fusion(bf16[1408,2,2048]{2,0,1:T(8,128)(2,1)} %all-gather.16.cloned.1.call-done, bf16[1024,2048]{1,0:T(8,128)(2,1)} %all-gather.14.cloned.1.call-done), kind=kOutput, calls=%fused_computation.4 | convolution fusion | flops 11811160064 | bytes 27262976 | tf_op jit(solution)/shard_map/td,fkd->tkf/dot_general | solution.py:140
  444.8 17.3 all-gather.18.cloned.1.call-done
  462.1 94.9 %all-gather.20.cloned.1.call-done = bf16[1408,2048]{1,0:T(8,128)(2,1)} async-done(((bf16[176,2048]{1,0:T(8,128)(2,1)}), bf16[1408,2048]{1,0:T(8,128)(2,1)}) %all-gather.20.cloned.1.call-update) | async-done | bytes 5767184 | tf_op jit(solution)/shard_map/all_gather | solution.py:152
  557.0 15.6 fusion.13
  572.6 1.6 copy-done.35
  575.1 16.3 bitcast_convert_fusion
  592.5 4.2 collective-permute-start.1
  596.6 26.3 %collective-permute-done = bf16[176,2048]{1,0:T(8,128)(2,1)} collective-permute-done((bf16[176,2048]{1,0:T(8,128)(2,1)}, bf16[176,2048]{1,0:T(8,128)(2,1)}, u32[]{:S(2)}, u32[]{:S(2)}) %collective-permute-start) | collective-permute-done | bytes 720928 | tf_op jit(solution)/shard_map/ppermute | solution.py:21
  622.9 2.5 collective-permute-start.2
  625.4 2.2 collective-permute-start.3
  628.5 26.8 %collective-permute-done.2 = bf16[176,2048]{1,0:T(8,128)(2,1)} collective-permute-done((bf16[176,2048]{1,0:T(8,128)(2,1)}, bf16[176,2048]{1,0:T(8,128)(2,1)}, u32[]{:S(2)}, u32[]{:S(2)}) %collective-permute-start.2) | collective-permute-done | bytes 720928 | tf_op jit(solution)/shard_map/ppermute | solution.py:21
  655.3 2.5 collective-permute-start.4
  659.0 1.3 constant_dynamic-update-slice_fusion.5
  660.3 2.5 collective-permute-start.5
  664.0 23.6 %collective-permute-done.4 = bf16[176,2048]{1,0:T(8,128)(2,1)S(1)} collective-permute-done((bf16[176,2048]{1,0:T(8,128)(2,1)}, bf16[176,2048]{1,0:T(8,128)(2,1)S(1)}, u32[]{:S(2)}, u32[]{:S(2)}) %collective-permute-start.4) | collective-permute-done | bytes 720928 | tf_op jit(solution)/shard_map/ppermute | solution.py:21
  687.6 2.4 collective-permute-start.6
  690.6 15.3 collective-permute-done.6
  706.0 8.3 convolution_convert_fusion.1
  714.4 10.5 convolution_convert_fusion
  725.2 18.3 %convert_bitcast_fusion = bf16[1408,2,2048]{0,2,1:T(8,128)(2,1)} fusion(bf16[1024,2048]{1,0:T(8,128)(2,1)} %all-gather.14.cloned.1.call-done, bf16[1024,1,1408]{2,0,1:T(8,128)(2,1)} %copy-done.36, bf16[1024,1,1408]{2,0,1:T(8,128)(2,1)} %copy-done.35), kind=kOutput, calls=%fused_computation.1 | convolution fusion | flops 11828461568 | bytes 21495808 | tf_op jit(solution)/shard_map/tkf,td->fkd/dot_general | solution.py:172
  743.5 29.2 %copy.89 = bf16[1408,2,2048]{2,1,0:T(2,128)(2,1)} copy(bf16[1408,2,2048]{0,2,1:T(8,128)(2,1)} %convert_bitcast_fusion) | data formatting | bytes 23068672 | tf_op jit(solution)/shard_map/convert_element_type | solution.py:172
  774.3 1.6 convert_multiply_fusion.5
  775.9 1.4 log_add_fusion
  777.3 2.6 fusion.19
  779.9 4.4 fusion.18
  784.3 1.3 copy-done.2
  785.6 6.8 convolution_convert_fusion.2
  792.4 1.8 copy.106
  794.2 3.6 fusion.61
  797.8 9.3 fusion.49
  808.4 9.5 fusion.35
  818.0 3.0 subtract_convert_fusion
  821.0 1.6 pad_maximum_fusion.4
  822.5 1.5 copy.82
  824.0 4.2 fusion.85
  828.2 8.1 fusion.37
  836.6 1.3 copy-done.3
  837.9 9.6 fusion.53
  853.0 6.2 fusion.88
  859.2 2.3 fusion.25
  861.5 39.4 %all-reduce.5 = (f32[2048]{0:T(1024)S(1)}, f32[2048]{0:T(1024)S(1)}) all-reduce(f32[2048]{0:T(1024)S(1)} %get-tuple-element.46, f32[2048]{0:T(1024)S(1)} %copy-done.26), channel_id=5, replica_groups=mesh['dp'=4,'fsdp'=8] {'dp','fsdp'}, use_global_device_ids=true, to_apply=%region_12.13.clone | all-reduce | flops 4096 | bytes 32768
  902.1 3.5 fusion.24
  905.5 2.4 convert_element_type.122
  907.9 323.1 %all-reduce.9.cloned.1.call-done = bf16[1408,2,2048]{2,1,0:T(2,128)(2,1)} async-done(((bf16[1408,2,2048]{2,1,0:T(2,128)(2,1)}), bf16[1408,2,2048]{2,1,0:T(2,128)(2,1)}) %all-reduce.9.cloned.1.call-update) | async-done | bytes 11534352
  1231.0 4.6 dynamic-slice_convert_fusion
  1235.7 207.4 %reduce-scatter.10.cloned.1.call-done = f32[64,2304]{1,0:T(8,128)} async-done(((f32[2048,2304]{1,0:T(8,128)}), f32[64,2304]{1,0:T(8,128)}) %reduce-scatter.10.cloned.1.call-update) | async-done | bytes 589840 | tf_op jit(solution)/shard_map/reduce_scatter | solution.py:224
  1443.1 1.9 slice.77
  1445.0 1.5 slice.78
  1446.4 356.5 %reduce-scatter.12.cloned.1.call-done = f32[64,2048]{1,0:T(8,128)} async-done(((f32[2048,2048]{1,0:T(8,128)}), f32[64,2048]{1,0:T(8,128)}) %reduce-scatter.12.cloned.1.call-update) | async-done | bytes 524304 | tf_op jit(solution)/shard_map/reduce_scatter | solution.py:188
  (143 shorter events, 23.9 us)
Async XLA Ops:
  7.2 5.4 copy-start.31
  7.2 5.7 copy-start.32
  7.2 48.7 %copy-start.1 = (bf16[256,2048]{1,0:T(8,128)(2,1)S(1)}, bf16[256,2048]{1,0:T(8,128)(2,1)}, u32[]{:S(2)}) copy-start(bf16[256,2048]{1,0:T(8,128)(2,1)} %param.13) | copy-start | bytes 3145732
  7.2 60.6 %all-gather.8.cloned.1.call-start = ((), (), s32[]{:S(2)}) async-start(), calls=%async_computation.5 | async-start | bytes 1081344 | tf_op jit(solution)/shard_map/all_gather | solution.py:93
  7.9 139.1 %all-gather.10.cloned.1.call-start = ((), (), s32[]{:S(2)}) async-start(), calls=%async_computation.6 | async-start | bytes 8650752 | tf_op jit(solution)/shard_map/all_gather | solution.py:92
  8.7 217.4 %all-gather.12.cloned.1.call-start = ((), (), s32[]{:S(2)}) async-start(), calls=%async_computation.7 | async-start | bytes 8650752 | tf_op jit(solution)/shard_map/all_gather | solution.py:125
  9.4 381.5 %all-gather.16.cloned.1.call-start = ((), (), s32[]{:S(2)}) async-start(), calls=%async_computation.9 | async-start | bytes 12976128 | tf_op jit(solution)/shard_map/all_gather | solution.py:138
  12.5 413.1 %all-gather.14.cloned.1.call-start = ((), (), s32[]{:S(2)}) async-start(), calls=%async_computation.8 | async-start | bytes 5242880 | tf_op jit(solution)/shard_map/all_gather | solution.py:135
  55.2 91.8 %copy-start.14 = (f32[2048]{0:T(1024)}, f32[2048]{0:T(1024)S(1)}, u32[]{:S(2)}) copy-start(f32[2048]{0:T(1024)S(1)} %convert_element_type.95) | copy-start | bytes 24580
  55.8 14.3 copy-start.28
  56.2 90.9 %copy-start.24 = (f32[256]{0:T(256)}, f32[256]{0:T(256)S(1)}, u32[]{:S(2)}) copy-start(f32[256]{0:T(256)S(1)} %add_rsqrt_fusion.1) | copy-start | bytes 3076
  69.6 77.4 %copy-start.12 = (f32[256,256]{0,1:T(8,128)}, f32[256,256]{0,1:T(8,128)S(1)}, u32[]{:S(2)}) copy-start(f32[256,256]{0,1:T(8,128)S(1)} %fusion.81) | copy-start | bytes 786436
  70.0 85.3 %copy-start.16 = (bf16[256,64]{0,1:T(8,128)(2,1)}, bf16[256,64]{0,1:T(8,128)(2,1)S(1)}, u32[]{:S(2)}) copy-start(bf16[256,64]{0,1:T(8,128)(2,1)S(1)} %get-tuple-element.63) | copy-start | bytes 98308
  70.0 85.3 %copy-start.18 = (bf16[256,64]{0,1:T(8,128)(2,1)}, bf16[256,64]{0,1:T(8,128)(2,1)S(1)}, u32[]{:S(2)}) copy-start(bf16[256,64]{0,1:T(8,128)(2,1)S(1)} %get-tuple-element.64) | copy-start | bytes 98308
  155.2 2.0 copy-start.4
  155.3 2.0 copy-start.6
  155.3 3.3 copy-start.13
  156.6 2.0 copy-start
  158.6 2.0 copy-start.22
  226.1 6.2 copy-start.21
  232.2 2.0 copy-start.29
  232.2 2.0 copy-start.30
  232.3 212.5 %copy-start.27 = (f32[256]{0:T(256)}, f32[256]{0:T(256)S(1)}, u32[]{:S(2)}) copy-start(f32[256]{0:T(256)S(1)} %add_rsqrt_fusion) | copy-start | bytes 3076
  233.5 228.6 %all-gather.18.cloned.1.call-start = ((), (), s32[]{:S(2)}) async-start(), calls=%async_computation.11 | async-start | bytes 5242880 | tf_op jit(solution)/shard_map/all_gather | solution.py:136
  238.1 318.9 %all-gather.20.cloned.1.call-start = ((), (), s32[]{:S(2)}) async-start(), calls=%async_computation.12 | async-start | bytes 6488064 | tf_op jit(solution)/shard_map/all_gather | solution.py:152
  238.8 538.4 %reduce-scatter.8.cloned.1.call-start = ((), (), s32[]{:S(2)}) async-start(), calls=%async_computation.13 | async-start | bytes 5242880 | tf_op jit(solution)/shard_map/reduce_scatter | solution.py:162
  572.6 1.6 copy-start.35
  572.6 2.4 copy-start.36
  591.4 188.5 %reduce-scatter.6.cloned.1.call-start = ((), (), s32[]{:S(2)}) async-start(), calls=%async_computation.10 | async-start | bytes 5242880 | tf_op jit(solution)/shard_map/reduce_scatter | solution.py:148
  591.5 31.5 %collective-permute-start = (bf16[176,2048]{1,0:T(8,128)(2,1)}, bf16[176,2048]{1,0:T(8,128)(2,1)}, u32[]{:S(2)}, u32[]{:S(2)}) collective-permute-start(bf16[176,2048]{1,0:T(8,128)(2,1)} %param.20), channel_id=1, source_target_pairs={{0,1},{1,2},{2,3},{3,4},{4,5},{5,6},{6,7},{7,0},{8,9},{9,10},{10,1... | collective-permute-start | bytes 2162696 | tf_op jit(solution)/shard_map/ppermute | solution.py:21
  592.5 33.0 %collective-permute-start.1 = (bf16[176,2048]{1,0:T(8,128)(2,1)}, bf16[176,2048]{1,0:T(8,128)(2,1)}, u32[]{:S(2)}, u32[]{:S(2)}) collective-permute-start(bf16[176,2048]{1,0:T(8,128)(2,1)} %param.20), channel_id=1, source_target_pairs={{0,7},{1,0},{2,1},{3,2},{4,3},{5,4},{6,5},{7,6},{8,15},{9,8},{10,9... | collective-permute-start | bytes 2162696 | tf_op jit(solution)/shard_map/ppermute | solution.py:26
  622.9 32.3 %collective-permute-start.2 = (bf16[176,2048]{1,0:T(8,128)(2,1)}, bf16[176,2048]{1,0:T(8,128)(2,1)}, u32[]{:S(2)}, u32[]{:S(2)}) collective-permute-start(bf16[176,2048]{1,0:T(8,128)(2,1)} %collective-permute-done), channel_id=1, source_target_pairs={{0,1},{1,2},{2,3},{3,4},{4,5},{5,6},{6,7},{7,0},{8,9},{9,10},{10,1... | collective-permute-start | bytes 2162696 | tf_op jit(solution)/shard_map/ppermute | solution.py:21
  625.4 3.0 copy-start.8
  625.4 34.9 %collective-permute-start.3 = (bf16[176,2048]{1,0:T(8,128)(2,1)}, bf16[176,2048]{1,0:T(8,128)(2,1)S(1)}, u32[]{:S(2)}, u32[]{:S(2)}) collective-permute-start(bf16[176,2048]{1,0:T(8,128)(2,1)} %collective-permute-done.1), channel_id=1, source_target_pairs={{0,7},{1,0},{2,1},{3,2},{4,3},{5,4},{6,5},{7,6},{8,15},{9,8},{10,9... | collective-permute-start | bytes 2162696 | tf_op jit(solution)/shard_map/ppermute | solution.py:26
  655.3 32.3 %collective-permute-start.4 = (bf16[176,2048]{1,0:T(8,128)(2,1)}, bf16[176,2048]{1,0:T(8,128)(2,1)S(1)}, u32[]{:S(2)}, u32[]{:S(2)}) collective-permute-start(bf16[176,2048]{1,0:T(8,128)(2,1)} %collective-permute-done.2), channel_id=1, source_target_pairs={{0,1},{1,2},{2,3},{3,4},{4,5},{5,6},{6,7},{7,0},{8,9},{9,10},{10,1... | collective-permute-start | bytes 2162696 | tf_op jit(solution)/shard_map/ppermute | solution.py:21
  658.9 47.1 %copy-start.34 = (bf16[1024,1408]{1,0:T(8,128)(2,1)S(1)}, bf16[1024,1408]{1,0:T(8,128)(2,1)}, u32[]{:S(2)}) copy-start(bf16[1024,1408]{1,0:T(8,128)(2,1)} %get-tuple-element.54) | copy-start | bytes 8650756
  660.3 30.2 %collective-permute-start.5 = (bf16[176,2048]{1,0:T(8,128)(2,1)S(1)}, bf16[176,2048]{1,0:T(8,128)(2,1)S(1)}, u32[]{:S(2)}, u32[]{:S(2)}) collective-permute-start(bf16[176,2048]{1,0:T(8,128)(2,1)S(1)} %collective-permute-done.3), channel_id=1, source_target_pairs={{0,7},{1,0},{2,1},{3,2},{4,3},{5,4},{6,5},{7,6},{8,15},{9,8},{10,9... | collective-permute-start | bytes 2162696 | tf_op jit(solution)/shard_map/ppermute | solution.py:26
  687.6 18.3 %collective-permute-start.6 = (bf16[176,2048]{1,0:T(8,128)(2,1)S(1)}, bf16[176,2048]{1,0:T(8,128)(2,1)S(1)}, u32[]{:S(2)}, u32[]{:S(2)}) collective-permute-start(bf16[176,2048]{1,0:T(8,128)(2,1)S(1)} %collective-permute-done.4), channel_id=1, source_target_pairs={{0,1},{1,2},{2,3},{3,4},{4,5},{5,6},{6,7},{7,0},{8,9},{9,10},{10,1... | collective-permute-start | bytes 2162696 | tf_op jit(solution)/shard_map/ppermute | solution.py:21
  714.3 191.2 %reduce-scatter.14.cloned.1.call-start = ((), (), s32[]{:S(2)}) async-start(), calls=%async_computation.16 | async-start | bytes 6488064 | tf_op jit(solution)/shard_map/reduce_scatter | solution.py:165
  725.0 506.1 %all-reduce.9.cloned.1.call-start = ((), (), s32[]{:S(2)}) async-start(), calls=%async_computation.17 | async-start | bytes 23068672
  772.7 0.9 copy-start.20
  772.7 670.4 %reduce-scatter.10.cloned.1.call-start = ((), (), s32[]{:S(2)}) async-start(), calls=%async_computation.14 | async-start | bytes 19464192 | tf_op jit(solution)/shard_map/reduce_scatter | solution.py:224
  775.9 21.9 %copy-start.10 = (f32[256,256]{0,1:T(8,128)}, f32[256,256]{0,1:T(8,128)S(1)}, u32[]{:S(2)}) copy-start(f32[256,256]{0,1:T(8,128)S(1)} %convert_multiply_fusion.5) | copy-start | bytes 786436
  784.3 1.3 copy-start.2
  792.4 5.4 copy-start.5
  792.4 5.4 copy-start.23
  820.9 3.1 copy-start.11
  822.5 5.7 copy-start.15
  822.5 5.7 copy-start.25
  824.0 12.3 copy-start.7
  836.3 1.6 copy-start.3
  836.3 966.6 %reduce-scatter.12.cloned.1.call-start = ((), (), s32[]{:S(2)}) async-start(), calls=%async_computation.15 | async-start | bytes 17301504 | tf_op jit(solution)/shard_map/reduce_scatter | solution.py:188
  847.5 0.7 copy-start.33
  847.5 2.8 copy-start.17
  847.6 2.8 copy-start.19
  853.0 6.2 copy-start.9
  859.2 2.3 copy-start.26
Sparse Core Ops, SparseCore 0:
  11.1 56.5 all-gather.7
  70.7 76.2 all-gather.9
  150.0 75.9 all-gather.11
  228.7 162.2 all-gather.15
  392.9 32.6 all-gather.13
  427.6 34.4 all-gather.17
  464.3 92.6 all-gather.19
  591.5 42.6 reduce-scatter.7
  714.5 42.7 reduce-scatter.5
  760.8 109.9 reduce-scatter.13
  874.7 356.3 all-reduce.8
  1237.3 205.7 reduce-scatter.9
  1445.9 356.9 reduce-scatter.11
